TPU v7x, 32 devices: a whole 2x2x4 slice. The times are simulated.
32 devices in a mesh: groups: 2 (over y), seq: 16 (over z, x, core).
Axes of the slice: x: 2, y: 2, z: 4, core: 2. Of those that a mesh axis runs over, the one named last changes fastest.
Arguments:
- frames_in: bfloat16 [8192, 1024], P(('groups', 'seq')), parts along dimension 0, may hold values from -40 to 40
- rec_start: int32 [8192], P(('groups', 'seq')), parts along dimension 0, may hold values from 0 to 4095, as said below
- norm_attn: float32 [1024], replicated, may hold values from 0.1 to 1.9
- w_query: bfloat16 [1024, 1024], replicated, may hold values from -1 to 1
- w_key: bfloat16 [1024, 1024], replicated, may hold values from -1 to 1
- w_value: bfloat16 [1024, 1024], replicated, may hold values from -0.1875 to 0.1875
- w_out: bfloat16 [1024, 1024], replicated, may hold values from -0.1875 to 0.1875
- norm_conv: float32 [1024], replicated, may hold values from 0.1 to 1.9
- w_glu: bfloat16 [1024, 2048], replicated, may hold values from -0.1875 to 0.1875
- w_depth: float32 [31, 1024], replicated, may hold values from -1 to 1
- norm_depth: float32 [1024], replicated, may hold values from 0.1 to 1.9
Outputs:
- conv_out: bfloat16 [8192, 1024], P(('groups', 'seq')), parts along dimension 0
There are 2 independent parts, one for each index of `groups`. A program takes and returns all parts, laid end to end along the dimension named above; an argument that names none is the same for every part. Nothing has to cross between parts.
Inputs may be any that keep to these rules, and one draw needn't show every extreme that they name: Recordings lie end to end from frame 0; rec_start[i] is the first frame of the recording that holds frame i. Each recording has 213 to 1280 frames, except the last, which the slab's end may cut; one of the first two has exactly 1280 frames.
All inputs are finite; a program needn't handle non-finite values.
Results may differ from a plain program's by a relative error of at most 0.0065.
Values may be sent and summed in bfloat16 or wider, within the bound.
A program may use at most 128 MiB of HBM per device.

v0:
```python
import math

import jax
import jax.numpy as jnp
from jax import lax
from jax.sharding import PartitionSpec as P

HD = 64
KW = 31
HOPS = 5


EPSILON = 1e-05
FLOOR_SCORE = -1e30


def passed_along(block, axis, distance):
    devices = range(lax.axis_size(axis))
    route = [(i - distance, i) for i in devices if i - distance in devices]
    return lax.ppermute(block, axis, route)


def layer_norm(entries, scaling):
    entries = entries.astype(jnp.float32)
    center = entries - jnp.mean(entries, axis=-1, keepdims=True)
    spread = jnp.mean(center * center, axis=-1, keepdims=True)
    return center * lax.rsqrt(spread + EPSILON) * scaling


def gated_units(features, norm_conv, w_glu):
    normed_conv = layer_norm(features, norm_conv).astype(jnp.bfloat16)
    mixed = jnp.dot(normed_conv, w_glu, preferred_element_type=jnp.float32)
    feature_width = features.shape[1]
    return (mixed[:, :feature_width] * jax.nn.sigmoid(mixed[:, feature_width:])).astype(
        jnp.bfloat16
    )


def body(
    frames_in,
    rec_start,
    norm_attn,
    w_query,
    w_key,
    w_value,
    w_out,
    norm_conv,
    w_glu,
    w_depth,
    norm_depth,
):
    row_count = frames_in.shape[0]
    feature_width = frames_in.shape[1]
    head_count = feature_width // HD
    device_index = lax.axis_index("seq")
    hop_count = HOPS
    normed_in = layer_norm(frames_in, norm_attn).astype(jnp.bfloat16)
    query = jnp.dot(normed_in, w_query, preferred_element_type=jnp.float32).astype(jnp.bfloat16)
    key_rows = jnp.dot(normed_in, w_key, preferred_element_type=jnp.float32).astype(jnp.bfloat16)
    value_rows = jnp.dot(normed_in, w_value, preferred_element_type=jnp.float32).astype(
        jnp.bfloat16
    )
    paired_rows = jnp.concatenate([key_rows, value_rows], axis=1)

    def advance_hop(hop_index, running):
        moving_pairs, stored_pairs = running
        moving_pairs = passed_along(moving_pairs, "seq", 1)
        stored_pairs = lax.dynamic_update_slice_in_dim(
            stored_pairs, moving_pairs[None], hop_count - 1 - hop_index, 0
        )
        return (moving_pairs, stored_pairs)

    stored_pairs = jnp.zeros((hop_count + 1, row_count, 2 * feature_width), jnp.bfloat16)
    stored_pairs = stored_pairs.at[hop_count].set(paired_rows)
    stored_pairs = lax.fori_loop(0, hop_count, advance_hop, (paired_rows, stored_pairs))[1]
    group_size = max(1, (512 + row_count - 1) // row_count)
    slot_count = (hop_count + group_size) // group_size * group_size
    front_zeros = jnp.zeros(
        (slot_count - hop_count - 1, row_count, 2 * feature_width), jnp.bfloat16
    )
    stored_pairs = jnp.concatenate([front_zeros, stored_pairs], axis=0)
    block_rows = group_size * row_count
    key_blocks = stored_pairs.reshape(slot_count // group_size, block_rows, 2 * feature_width)
    query_heads = query.reshape(row_count, head_count, HD)
    query_places = device_index * row_count + jnp.arange(row_count, dtype=jnp.int32)
    first_place = (device_index - slot_count + 1) * row_count
    score_scale = 1.0 / math.sqrt(HD)

    def attend_block(block_index, running):
        highest, weight_sum, summed = running
        block_pairs = lax.dynamic_index_in_dim(key_blocks, block_index, 0, keepdims=False)
        key_places = (
            first_place + block_index * block_rows + jnp.arange(block_rows, dtype=jnp.int32)
        )
        visible = (key_places[None, :] >= rec_start[:, None]) & (
            key_places[None, :] <= query_places[:, None]
        )
        key_heads = block_pairs[:, :feature_width].reshape(block_rows, head_count, HD)
        value_heads = block_pairs[:, feature_width:].reshape(block_rows, head_count, HD)
        scores = (
            jnp.einsum("qhd,khd->hqk", query_heads, key_heads, preferred_element_type=jnp.float32)
            * score_scale
        )
        new_highest = jnp.maximum(
            highest, jnp.max(jnp.where(visible[None], scores, FLOOR_SCORE), axis=-1)
        )
        weights = jnp.where(visible[None], jnp.exp(scores - new_highest[:, :, None]), 0.0).astype(
            jnp.bfloat16
        )
        factor = jnp.exp(highest - new_highest)
        weight_sum = weight_sum * factor + jnp.sum(weights.astype(jnp.float32), axis=-1)
        summed = summed * factor.T[:, :, None] + jnp.einsum(
            "hqk,khd->qhd", weights, value_heads, preferred_element_type=jnp.float32
        )
        return (new_highest, weight_sum, summed)

    initial_state = (
        jnp.full((head_count, row_count), FLOOR_SCORE, jnp.float32),
        jnp.zeros((head_count, row_count), jnp.float32),
        jnp.zeros((row_count, head_count, HD), jnp.float32),
    )
    final_state = lax.fori_loop(0, slot_count // group_size, attend_block, initial_state)
    heads_out = (
        (final_state[2] / final_state[1].T[:, :, None])
        .reshape(row_count, feature_width)
        .astype(jnp.bfloat16)
    )
    attn_res = (
        frames_in.astype(jnp.float32)
        + jnp.dot(heads_out, w_out, preferred_element_type=jnp.float32)
    ).astype(jnp.bfloat16)
    gated = gated_units(attn_res, norm_conv, w_glu)
    rim_rows = passed_along(gated[row_count - KW + 1 :], "seq", 1)
    extended = jnp.concatenate([rim_rows, gated], axis=0)
    depth = jnp.zeros((row_count, feature_width), jnp.float32)
    for tap_index in range(KW):
        source = query_places - (KW - 1) + tap_index
        keep = (source >= rec_start)[:, None]
        depth = (
            depth
            + jnp.where(keep, extended[tap_index : tap_index + row_count].astype(jnp.float32), 0.0)
            * w_depth[tap_index]
        )
    normed_depth = layer_norm(depth, norm_depth)
    return (attn_res.astype(jnp.float32) + normed_depth * jax.nn.sigmoid(normed_depth)).astype(
        jnp.bfloat16
    )


def solution(mesh):
    return jax.shard_map(
        body,
        mesh=mesh,
        in_specs=(
            P(("groups", "seq"), None),
            P(("groups", "seq")),
            P(),
            P(),
            P(),
            P(),
            P(),
            P(),
            P(),
            P(),
            P(),
        ),
        out_specs=P(("groups", "seq"), None),
        check_vma=False,
    )
```

profile of v0, /device:TPU:8, one launch (start us, length us, event | category | flops | bytes accessed | tf_op | source)
XLA Modules:
  0.0 199.2 jit_solution(15724310727418218606)
XLA Ops:
  2.9 3.3 %convolution_convert_fusion.1 = bf16[256,1024]{1,0:T(8,128)(2,1)} fusion(bf16[1024,1024]{1,0:T(8,128)(2,1)} %param.22, bf16[256,1024]{1,0:T(8,128)(2,1)} %param.17, f32[1024]{0:T(1024)} %param.19, f32[256]{0:T(256)S(1)} %add_rsqrt_fusion.2, f32[256]{0:T(256)S(1)} %broadcast_multiply_fusion.2), kind=kOutput, calls=%fused_computation.60 | convolution fusion | flops 538443776 | bytes 3151872 | tf_op jit(solution)/shard_map/dot_general | solution.py:60
  9.6 2.3 %fusion.64 = (bf16[1,256,2048]{2,1,0:T(8,128)(2,1)S(1)}, bf16[256,2048]{1,0:T(8,128)(2,1)}) fusion(bf16[256,1024]{1,0:T(8,128)(2,1)} %convolution_convert_fusion.1, bf16[256,1024]{1,0:T(8,128)(2,1)} %convolution_convert_fusion.2), kind=kLoop, calls=%fused_computation.163 | loop fusion | flops 2097152 | bytes 3145728 | tf_op jit(solution)/shard_map/reshape.43
  11.9 3.5 %scatter.4 = bf16[6,256,2048]{2,1,0:T(8,128)(2,1)} pad(bf16[1,256,2048]{2,1,0:T(8,128)(2,1)S(1)} %get-tuple-element.322, bf16[]{:T(256)} %constant.198.clone.1), padding=5_0x0_0x0_0 | pad | bytes 7340034 | tf_op jit(solution)/shard_map/scatter | solution.py:74
  15.4 96.4 %while.34 = (s32[]{:T(128)}, bf16[256,2048]{1,0:T(8,128)(2,1)}, bf16[6,256,2048]{2,1,0:T(8,128)(2,1)}, s32[]{:T(128)}, s32[]{:T(128)}, /*index=5*/s32[]{:T(128)}, s32[]{:T(128)}) while((s32[]{:T(128)}, bf16[256,2048]{1,0:T(8,128)(2,1)}, bf16[6,256,2048]{2,1,0:T(8,128)(2,1)}, s32[]{:T(128)}, s32[]{:T(128)}, /*index=5*/s32[]{:T(128)}, ...), condition=%wide.region_3.0_spmd, body=%wide.region_2.0_spmd.sunk | while | flops 6 | bytes 8388775 | solution.py:75
  17.5 15.3 %collective-permute-done = bf16[256,2048]{1,0:T(8,128)(2,1)S(1)} collective-permute-done((bf16[256,2048]{1,0:T(8,128)(2,1)}, bf16[256,2048]{1,0:T(8,128)(2,1)S(1)}, u32[]{:S(2)}, u32[]{:S(2)}) %collective-permute-start) | collective-permute-done | bytes 1048608 | tf_op jit(solution)/shard_map/while/body/eval_jaxpr/ppermute | solution.py:20
  36.8 15.3 %collective-permute-done = bf16[256,2048]{1,0:T(8,128)(2,1)S(1)} collective-permute-done((bf16[256,2048]{1,0:T(8,128)(2,1)}, bf16[256,2048]{1,0:T(8,128)(2,1)S(1)}, u32[]{:S(2)}, u32[]{:S(2)}) %collective-permute-start) | collective-permute-done | bytes 1048608 | tf_op jit(solution)/shard_map/while/body/eval_jaxpr/ppermute | solution.py:20
  56.0 15.3 %collective-permute-done = bf16[256,2048]{1,0:T(8,128)(2,1)S(1)} collective-permute-done((bf16[256,2048]{1,0:T(8,128)(2,1)}, bf16[256,2048]{1,0:T(8,128)(2,1)S(1)}, u32[]{:S(2)}, u32[]{:S(2)}) %collective-permute-start) | collective-permute-done | bytes 1048608 | tf_op jit(solution)/shard_map/while/body/eval_jaxpr/ppermute | solution.py:20
  75.2 15.3 %collective-permute-done = bf16[256,2048]{1,0:T(8,128)(2,1)S(1)} collective-permute-done((bf16[256,2048]{1,0:T(8,128)(2,1)}, bf16[256,2048]{1,0:T(8,128)(2,1)S(1)}, u32[]{:S(2)}, u32[]{:S(2)}) %collective-permute-start) | collective-permute-done | bytes 1048608 | tf_op jit(solution)/shard_map/while/body/eval_jaxpr/ppermute | solution.py:20
  94.5 15.3 %collective-permute-done = bf16[256,2048]{1,0:T(8,128)(2,1)S(1)} collective-permute-done((bf16[256,2048]{1,0:T(8,128)(2,1)}, bf16[256,2048]{1,0:T(8,128)(2,1)S(1)}, u32[]{:S(2)}, u32[]{:S(2)}) %collective-permute-start) | collective-permute-done | bytes 1048608 | tf_op jit(solution)/shard_map/while/body/eval_jaxpr/ppermute | solution.py:20
  111.8 65.8 %while.35 = (s32[]{:T(128)}, f32[16,256]{1,0:T(8,128)S(1)}, f32[16,256]{1,0:T(8,128)S(1)}, f32[256,16,64]{0,2,1:T(8,128)}, s32[]{:T(128)}, /*index=5*/s32[256]{0...) while((s32[]{:T(128)}, f32[16,256]{1,0:T(8,128)S(1)}, ...), condition=%wide.region_7.8_spmd.clone, body=%wide.region_4.7_spmd.clone.sunk | while | flops 565338880 | bytes 78912728 | solution.py:122
  112.0 3.2 %constant_dynamic-slice_fusion.2 = bf16[1,512,2048]{2,1,0:T(8,128)(2,1)} fusion(bf16[3,512,2048]{2,1,0:T(8,128)(2,1)} %get-tuple-element.525, s32[]{:T(128)} %get-tuple-element.507), kind=kLoop, calls=%fused_computation.20.clone.1 | loop fusion | bytes 4194308 | tf_op jit(solution)/shard_map/while/body/eval_jaxpr/jit(dynamic_index_in_dim)/dynamic_slice | solution.py:91
  115.2 3.9 %copy.20 = bf16[1,512,2048]{1,2,0:T(8,128)(2,1)} copy(bf16[1,512,2048]{2,1,0:T(8,128)(2,1)} %constant_dynamic-slice_fusion.2) | data formatting | bytes 4194304 | tf_op jit(solution)/shard_map/while/body/eval_jaxpr/jit(dynamic_index_in_dim)/dynamic_slice | solution.py:91
  120.9 4.7 %fusion.95 = (f32[16,256]{1,0:T(8,128)S(1)}, f32[16,512,256]{2,1,0:T(8,128)}) fusion(pred[256,512]{0,1:T(8,128)(4,1)S(1)} %compare_and_fusion.2, bf16[512,16,64]{0,2,1:T(8,128)(2,1)S(1)} %bitcast.96, bf16[256,16,64]{0,2,1:T(8,128)(2,1)S(1)} %copy-done.2), kind=kOutput, calls=%fused_computation.4.clone.1 | convolution fusion | flops 274722816 | bytes 10108928 | tf_op jit(solution)/shard_map/while/body/eval_jaxpr/qhd,khd->hqk/dot_general | solution.py:101
  125.6 6.3 %fusion.98 = f32[256,16,64]{0,2,1:T(8,128)} fusion(bf16[512,16,64]{0,2,1:T(8,128)(2,1)S(1)} %bitcast.98, f32[256,16,64]{0,2,1:T(8,128)} %get-tuple-element.510, f32[256,16]{0,1:T(8,128)S(1)} %get-tuple-element.473, pred[]{:T(512)S(6)} %compare.9, f32[16,512,256]{2,1,0:T(8,128)} %get-tuple-element.471, f32[16,256]{1,0:T(8,128)S(1)} %get-tuple-element.520, ...), kind=kOutput, calls=%fused_computation.10.clone.1 | convolution fusion | flops 277610496 | bytes 11698177 | tf_op jit(solution)/shard_map/while/body/eval_jaxpr/hqk,khd->qhd/dot_general | solution.py:112
  133.8 3.2 %constant_dynamic-slice_fusion.2 = bf16[1,512,2048]{2,1,0:T(8,128)(2,1)} fusion(bf16[3,512,2048]{2,1,0:T(8,128)(2,1)} %get-tuple-element.525, s32[]{:T(128)} %get-tuple-element.507), kind=kLoop, calls=%fused_computation.20.clone.1 | loop fusion | bytes 4194308 | tf_op jit(solution)/shard_map/while/body/eval_jaxpr/jit(dynamic_index_in_dim)/dynamic_slice | solution.py:91
  137.0 3.9 %copy.20 = bf16[1,512,2048]{1,2,0:T(8,128)(2,1)} copy(bf16[1,512,2048]{2,1,0:T(8,128)(2,1)} %constant_dynamic-slice_fusion.2) | data formatting | bytes 4194304 | tf_op jit(solution)/shard_map/while/body/eval_jaxpr/jit(dynamic_index_in_dim)/dynamic_slice | solution.py:91
  142.7 4.7 %fusion.95 = (f32[16,256]{1,0:T(8,128)S(1)}, f32[16,512,256]{2,1,0:T(8,128)}) fusion(pred[256,512]{0,1:T(8,128)(4,1)S(1)} %compare_and_fusion.2, bf16[512,16,64]{0,2,1:T(8,128)(2,1)S(1)} %bitcast.96, bf16[256,16,64]{0,2,1:T(8,128)(2,1)S(1)} %copy-done.2), kind=kOutput, calls=%fused_computation.4.clone.1 | convolution fusion | flops 274722816 | bytes 10108928 | tf_op jit(solution)/shard_map/while/body/eval_jaxpr/qhd,khd->hqk/dot_general | solution.py:101
  147.4 6.5 %fusion.98 = f32[256,16,64]{0,2,1:T(8,128)} fusion(bf16[512,16,64]{0,2,1:T(8,128)(2,1)S(1)} %bitcast.98, f32[256,16,64]{0,2,1:T(8,128)} %get-tuple-element.510, f32[256,16]{0,1:T(8,128)S(1)} %get-tuple-element.473, pred[]{:T(512)S(6)} %compare.9, f32[16,512,256]{2,1,0:T(8,128)} %get-tuple-element.471, f32[16,256]{1,0:T(8,128)S(1)} %get-tuple-element.520, ...), kind=kOutput, calls=%fused_computation.10.clone.1 | convolution fusion | flops 277610496 | bytes 11698177 | tf_op jit(solution)/shard_map/while/body/eval_jaxpr/hqk,khd->qhd/dot_general | solution.py:112
  155.9 3.2 %constant_dynamic-slice_fusion.2 = bf16[1,512,2048]{2,1,0:T(8,128)(2,1)} fusion(bf16[3,512,2048]{2,1,0:T(8,128)(2,1)} %get-tuple-element.525, s32[]{:T(128)} %get-tuple-element.507), kind=kLoop, calls=%fused_computation.20.clone.1 | loop fusion | bytes 4194308 | tf_op jit(solution)/shard_map/while/body/eval_jaxpr/jit(dynamic_index_in_dim)/dynamic_slice | solution.py:91
  159.0 3.9 %copy.20 = bf16[1,512,2048]{1,2,0:T(8,128)(2,1)} copy(bf16[1,512,2048]{2,1,0:T(8,128)(2,1)} %constant_dynamic-slice_fusion.2) | data formatting | bytes 4194304 | tf_op jit(solution)/shard_map/while/body/eval_jaxpr/jit(dynamic_index_in_dim)/dynamic_slice | solution.py:91
  164.7 4.7 %fusion.95 = (f32[16,256]{1,0:T(8,128)S(1)}, f32[16,512,256]{2,1,0:T(8,128)}) fusion(pred[256,512]{0,1:T(8,128)(4,1)S(1)} %compare_and_fusion.2, bf16[512,16,64]{0,2,1:T(8,128)(2,1)S(1)} %bitcast.96, bf16[256,16,64]{0,2,1:T(8,128)(2,1)S(1)} %copy-done.2), kind=kOutput, calls=%fused_computation.4.clone.1 | convolution fusion | flops 274722816 | bytes 10108928 | tf_op jit(solution)/shard_map/while/body/eval_jaxpr/qhd,khd->hqk/dot_general | solution.py:101
  169.5 6.5 %fusion.98 = f32[256,16,64]{0,2,1:T(8,128)} fusion(bf16[512,16,64]{0,2,1:T(8,128)(2,1)S(1)} %bitcast.98, f32[256,16,64]{0,2,1:T(8,128)} %get-tuple-element.510, f32[256,16]{0,1:T(8,128)S(1)} %get-tuple-element.473, pred[]{:T(512)S(6)} %compare.9, f32[16,512,256]{2,1,0:T(8,128)} %get-tuple-element.471, f32[16,256]{1,0:T(8,128)S(1)} %get-tuple-element.520, ...), kind=kOutput, calls=%fused_computation.10.clone.1 | convolution fusion | flops 277610496 | bytes 11698177 | tf_op jit(solution)/shard_map/while/body/eval_jaxpr/hqk,khd->qhd/dot_general | solution.py:112
  185.5 4.2 %collective-permute-done.1 = bf16[30,1024]{1,0:T(8,128)(2,1)S(1)} collective-permute-done((bf16[30,1024]{1,0:T(8,128)(2,1)S(1)}, bf16[30,1024]{1,0:T(8,128)(2,1)S(1)}, u32[]{:S(2)}, u32[]{:S(2)}) %collective-permute-start.1) | collective-permute-done | bytes 61472 | tf_op jit(solution)/shard_map/ppermute | solution.py:20
  189.7 8.0 %fusion.68 = (f32[256]{0:T(256)S(1)}, f32[256,1024]{1,0:T(8,128)S(1)}) fusion(f32[1024]{0:T(1024)S(1)} %bitcast.131, bf16[256,1024]{1,0:T(8,128)(2,1)S(1)} %fusion.28, pred[256]{0:T(512)(128)(4,1)S(1)} %get-tuple-element.384, f32[1024]{0:T(1024)S(1)} %bitcast.132, bf16[30,1024]{1,0:T(8,128)(2,1)S(1)} %collective-permute-done.1, ...), kind=kLoop, calls=%fused_computation.164 | loop fusion | flops 56098560 | bytes 1770240 | tf_op jit(solution)/shard_map/reduce_sum | solution.py:25
  (97 shorter events, 46.2 us)
Async XLA Ops:
  0.0 179.2 %copy-start = (bf16[1024,1024]{1,0:T(8,128)(2,1)S(1)}, bf16[1024,1024]{1,0:T(8,128)(2,1)}, u32[]{:S(2)}) copy-start(bf16[1024,1024]{1,0:T(8,128)(2,1)} %param.23) | copy-start | bytes 6291460
  0.0 6.2 %copy-start.3 = (bf16[256,1024]{1,0:T(8,128)(2,1)S(1)}, bf16[256,1024]{1,0:T(8,128)(2,1)}, u32[]{:S(2)}) copy-start(bf16[256,1024]{1,0:T(8,128)(2,1)} %param.17) | copy-start | bytes 1572868
  0.0 6.2 %copy-start.10 = (f32[1024]{0:T(1024)S(1)}, f32[1024]{0:T(1024)}, u32[]{:S(2)}) copy-start(f32[1024]{0:T(1024)} %param.19) | copy-start | bytes 12292
  0.0 6.2 %copy-start.8 = (bf16[1024,1024]{1,0:T(8,128)(2,1)S(1)}, bf16[1024,1024]{1,0:T(8,128)(2,1)}, u32[]{:S(2)}) copy-start(bf16[1024,1024]{1,0:T(8,128)(2,1)} %param.21) | copy-start | bytes 6291460
  1.4 6.4 %copy-start.9 = (bf16[1024,1024]{1,0:T(8,128)(2,1)S(1)}, bf16[1024,1024]{1,0:T(8,128)(2,1)}, u32[]{:S(2)}) copy-start(bf16[1024,1024]{1,0:T(8,128)(2,1)} %param.20) | copy-start | bytes 6291460
  15.4 96.4 %copy-start.5 = (s32[256]{0:T(256)S(1)}, s32[256]{0:T(256)}, u32[]{:S(2)}) copy-start(s32[256]{0:T(256)} %param.18) | copy-start | bytes 3076
  15.4 17.3 %collective-permute-start = (bf16[256,2048]{1,0:T(8,128)(2,1)}, bf16[256,2048]{1,0:T(8,128)(2,1)S(1)}, u32[]{:S(2)}, u32[]{:S(2)}) collective-permute-start(bf16[256,2048]{1,0:T(8,128)(2,1)} %get-tuple-element.482), channel_id=1, source_target_pairs={{0,1},{1,2},{2,3},{3,4},{4,5},{5,6},{6,7},{7,8},{8,9},{9,10},{10,1... | collective-permute-start | bytes 3145736 | tf_op jit(solution)/shard_map/while/body/eval_jaxpr/ppermute | solution.py:20
  34.8 17.2 %collective-permute-start = (bf16[256,2048]{1,0:T(8,128)(2,1)}, bf16[256,2048]{1,0:T(8,128)(2,1)S(1)}, u32[]{:S(2)}, u32[]{:S(2)}) collective-permute-start(bf16[256,2048]{1,0:T(8,128)(2,1)} %get-tuple-element.482), channel_id=1, source_target_pairs={{0,1},{1,2},{2,3},{3,4},{4,5},{5,6},{6,7},{7,8},{8,9},{9,10},{10,1... | collective-permute-start | bytes 3145736 | tf_op jit(solution)/shard_map/while/body/eval_jaxpr/ppermute | solution.py:20
  54.1 17.2 %collective-permute-start = (bf16[256,2048]{1,0:T(8,128)(2,1)}, bf16[256,2048]{1,0:T(8,128)(2,1)S(1)}, u32[]{:S(2)}, u32[]{:S(2)}) collective-permute-start(bf16[256,2048]{1,0:T(8,128)(2,1)} %get-tuple-element.482), channel_id=1, source_target_pairs={{0,1},{1,2},{2,3},{3,4},{4,5},{5,6},{6,7},{7,8},{8,9},{9,10},{10,1... | collective-permute-start | bytes 3145736 | tf_op jit(solution)/shard_map/while/body/eval_jaxpr/ppermute | solution.py:20
  73.3 17.2 %collective-permute-start = (bf16[256,2048]{1,0:T(8,128)(2,1)}, bf16[256,2048]{1,0:T(8,128)(2,1)S(1)}, u32[]{:S(2)}, u32[]{:S(2)}) collective-permute-start(bf16[256,2048]{1,0:T(8,128)(2,1)} %get-tuple-element.482), channel_id=1, source_target_pairs={{0,1},{1,2},{2,3},{3,4},{4,5},{5,6},{6,7},{7,8},{8,9},{9,10},{10,1... | collective-permute-start | bytes 3145736 | tf_op jit(solution)/shard_map/while/body/eval_jaxpr/ppermute | solution.py:20
  92.5 17.2 %collective-permute-start = (bf16[256,2048]{1,0:T(8,128)(2,1)}, bf16[256,2048]{1,0:T(8,128)(2,1)S(1)}, u32[]{:S(2)}, u32[]{:S(2)}) collective-permute-start(bf16[256,2048]{1,0:T(8,128)(2,1)} %get-tuple-element.482), channel_id=1, source_target_pairs={{0,1},{1,2},{2,3},{3,4},{4,5},{5,6},{6,7},{7,8},{8,9},{9,10},{10,1... | collective-permute-start | bytes 3145736 | tf_op jit(solution)/shard_map/while/body/eval_jaxpr/ppermute | solution.py:20
  119.1 1.7 copy-start.2
  125.6 6.3 %copy-start.1 = (f32[16,512,256]{2,1,0:T(8,128)S(1)}, f32[16,512,256]{2,1,0:T(8,128)}, u32[]{:S(2)}) copy-start(f32[16,512,256]{2,1,0:T(8,128)} %get-tuple-element.471) | copy-start | bytes 25165828 | tf_op jit(solution)/shard_map/while
  140.9 1.7 copy-start.2
  147.4 6.5 %copy-start.1 = (f32[16,512,256]{2,1,0:T(8,128)S(1)}, f32[16,512,256]{2,1,0:T(8,128)}, u32[]{:S(2)}) copy-start(f32[16,512,256]{2,1,0:T(8,128)} %get-tuple-element.471) | copy-start | bytes 25165828 | tf_op jit(solution)/shard_map/while
  163.0 1.7 copy-start.2
  169.4 6.5 %copy-start.1 = (f32[16,512,256]{2,1,0:T(8,128)S(1)}, f32[16,512,256]{2,1,0:T(8,128)}, u32[]{:S(2)}) copy-start(f32[16,512,256]{2,1,0:T(8,128)} %get-tuple-element.471) | copy-start | bytes 25165828 | tf_op jit(solution)/shard_map/while
  177.7 3.8 %copy-start.7 = (bf16[1024,2048]{1,0:T(8,128)(2,1)S(1)}, bf16[1024,2048]{1,0:T(8,128)(2,1)}, u32[]{:S(2)}) copy-start(bf16[1024,2048]{1,0:T(8,128)(2,1)} %param.25) | copy-start | bytes 12582916
  177.7 3.8 %copy-start.11 = (f32[1024]{0:T(1024)S(1)}, f32[1024]{0:T(1024)}, u32[]{:S(2)}) copy-start(f32[1024]{0:T(1024)} %param.24) | copy-start | bytes 12292
  181.5 3.8 %copy-start.4 = (f32[31,1024]{1,0:T(8,128)S(1)}, f32[31,1024]{1,0:T(8,128)}, u32[]{:S(2)}) copy-start(f32[31,1024]{1,0:T(8,128)} %param.26) | copy-start | bytes 380932
  182.9 15.1 %copy-start.6 = (f32[1024]{0:T(1024)S(1)}, f32[1024]{0:T(1024)}, u32[]{:S(2)}) copy-start(f32[1024]{0:T(1024)} %param.27) | copy-start | bytes 12292
  183.2 6.5 %collective-permute-start.1 = (bf16[30,1024]{1,0:T(8,128)(2,1)S(1)}, bf16[30,1024]{1,0:T(8,128)(2,1)S(1)}, u32[]{:S(2)}, u32[]{:S(2)}) collective-permute-start(bf16[30,1024]{1,0:T(8,128)(2,1)S(1)} %slice.295), channel_id=1, source_target_pairs={{0,1},{1,2},{2,3},{3,4},{4,5},{5,6},{6,7},{7,8},{8,9},{9,10},{10,1... | collective-permute-start | bytes 184328 | tf_op jit(solution)/shard_map/ppermute | solution.py:20
where the time goes:
time: 200 us; the launch traced here: 199 us
  waiting for transfers between devices  80.6 us (40%)
  matrix products  42.4 us (21%)
  local copies, waits for them, and re-layouts  41.4 us (21%)
  other arithmetic  22.4 us (11%)
  starting transfers between devices  11.8 us (6%)
    ppermute x6, waiting for transfers between devices, passed_along(): return lax.ppermute(block, axis, route)  80.6 us
    dynamic_slice x6, local copies, waits for them, and re-layouts, attend_block(): lax.dynamic_index_in_dim(key_blocks, block_index, 0, keepdims=False)  21.3 us
    dot_general x3, matrix products, attend_block(): jnp.einsum('hqk,khd->qhd', weights, value_heads, preferred_element_type=j...  19.2 us
    dot_general x3, matrix products, attend_block(): jnp.einsum('qhd,khd->hqk', query_heads, key_heads, preferred_element_type...  14.1 us
    ppermute x6, starting transfers between devices, passed_along(): return lax.ppermute(block, axis, route)  11.8 us
    reduce_sum x2, other arithmetic, layer_norm(): center = entries - jnp.mean(entries, axis=-1, keepdims=True)  9.3 us
    dynamic_update_slice x5, local copies, waits for them, and re-layouts, advance_hop(): lax.dynamic_update_slice_in_dim(stored_pairs, moving_pairs[None], hop_cou...  5.32 us
    slice x3, local copies, waits for them, and re-layouts, attend_block(): block_pairs[:, feature_width:].reshape(block_rows, head_count, HD)  5.2 us
  transfers between devices with their start and end apart: 6, of which 6 were waited for; matrix products, arithmetic and copies ran while one was open for 0% of the time, Pallas kernels for 0%

commit v1 on v0

v1 whole, which is shorter than its diff:
```python
import jax
import jax.numpy as jnp
from jax import lax
from jax.experimental import pallas as pl
from jax.experimental.pallas import tpu as pltpu
from jax.sharding import PartitionSpec as P

HD = 64
KW = 31
EPSILON = 1e-05
FLOOR_SCORE = -1e30
F32 = jnp.float32
BF16 = jnp.bfloat16
MESH = pl.DeviceIdType.MESH
PIECES = 2
PLACE = {4: 0, 2: 1, 1: 2, 3: 3, 5: 4}
DISTANCE = (4, 2, 1, 3, 5)
A, B, C, D, E, F, G, H, I = range(9)


def layer_norm(entries, scaling):
    center = entries - jnp.mean(entries, axis=-1, keepdims=True)
    spread = jnp.mean(center * center, axis=-1, keepdims=True)
    return center * lax.rsqrt(spread + EPSILON) * scaling


def kernel(
    x_ref, start_ref, na_ref, nc_ref, nd_ref, wd_ref,
    wq_hbm, wk_hbm, wv_hbm, wo_hbm, wg_hbm,
    out_ref,
    xb, wq, wk, wv, wo, wg, xn, q2, kb, vb, bias, bias_own, startb, mx, acc, heads,
    res, gb, halo, gext, depth,
    w_sem, send_sem, recv_sem, halo_sem,
):
    n = lax.axis_size("seq")
    me = lax.axis_index("seq")
    p = me % 4
    rows, width = x_ref.shape
    piece = rows // PIECES
    pairs = width // 128

    barrier = pltpu.get_barrier_semaphore()
    peers = jnp.int32(0)
    for delta in (-4, -3, -2, -1, 1, 2, 3, 4):
        inside = (me + delta >= 0) & (me + delta < n)
        peers = peers + jnp.where(inside, 1, 0)

        @pl.when(inside)
        def _():
            pl.semaphore_signal(
                barrier, inc=1, device_id={"seq": me + delta}, device_id_type=MESH
            )
    pl.semaphore_wait(barrier, peers)

    def move(event, part, source, target, distance):
        span = pl.ds(part * piece, piece)
        src = x_ref.at[span] if source is None else xb.at[PLACE[source], span]
        return pltpu.make_async_remote_copy(
            src_ref=src,
            dst_ref=xb.at[PLACE[distance], span],
            send_sem=send_sem.at[event, part],
            recv_sem=recv_sem.at[event, part],
            device_id={"seq": target},
            device_id_type=MESH,
        )

    even = p % 2 == 0
    sends = {
        A: [(me + 4 < n, None, me + 4, 4)],
        B: [(p < 2, None, me + 2, 2)],
        C: [(even, None, me + 1, 1)],
        D: [(p == 2, 2, me + 1, 3), (p == 3, 2, me - 1, 1)],
        E: [((me >= 4) & even, 4, me + 1, 5), ((me >= 4) & (p % 2 == 1), 4, me - 1, 3)],
        F: [((me >= 4) & (p >= 2), 4, me - 2, 2)],
        G: [((me >= 4) & (p == 0), 2, me + 1, 3), ((me >= 4) & (p == 1), 2, me - 1, 1)],
        H: [((p == 3) & (me + 3 < n), 2, me + 3, 5)],
        I: [((me >= 4) & (p == 1) & (me + 3 < n), 2, me + 3, 5)],
    }
    receipts = {
        A: [(me >= 4, 4)],
        B: [(p >= 2, 2)],
        C: [(p % 2 == 1, 1)],
        D: [(p == 3, 3), (p == 2, 1)],
        E: [((me >= 4) & (p % 2 == 1), 5), ((me >= 4) & even, 3)],
        F: [((me >= 4) & (p < 2), 2)],
        G: [((me >= 4) & (p == 1), 3), ((me >= 4) & (p == 0), 1)],
        H: [((me >= 4) & (p == 2), 5)],
        I: [((me >= 8) & (p == 0), 5)],
    }

    def start(event, part):
        for condition, source, target, distance in sends[event]:
            @pl.when(condition)
            def _():
                move(event, part, source, target, distance).start()

    def wait_sent(event, part):
        for condition, source, target, distance in sends[event]:
            @pl.when(condition)
            def _():
                move(event, part, source, target, distance).wait_send()

    def wait_here(event, part):
        for condition, distance in receipts[event]:
            @pl.when(condition)
            def _():
                move(event, part, None, me, distance).wait_recv()

    for part in range(PIECES):
        start(A, part)
        start(B, part)
    for part in range(PIECES):
        start(C, part)

    weights = [
        pltpu.make_async_copy(src, dst, w_sem.at[index])
        for index, (src, dst) in enumerate(
            ((wq_hbm, wq), (wk_hbm, wk), (wv_hbm, wv), (wo_hbm, wo), (wg_hbm, wg))
        )
    ]
    for copy in weights:
        copy.start()

    for distance in DISTANCE:
        @pl.when(me < distance)
        def _():
            xb[PLACE[distance]] = jnp.zeros((rows, width), BF16)

    column = jnp.broadcast_to(start_ref[...].astype(F32), (rows, rows)).T
    startb[...] = column[:, :128] - (me * rows).astype(F32)
    first = startb[...]
    lane = lax.broadcasted_iota(jnp.int32, (rows, 128), 1).astype(F32)
    row_index = lax.broadcasted_iota(jnp.int32, (rows, 128), 0).astype(F32)
    for tile in range(rows // 128):
        place = lane + float(tile * 128)
        seen = (place >= first) & (place <= row_index)
        bias_own[:, tile * 128:(tile + 1) * 128] = jnp.where(seen, 0.0, FLOOR_SCORE)
        for slot, distance in enumerate(DISTANCE):
            at = slot * rows + tile * 128
            bias[:, at:at + 128] = jnp.where(
                place - float(distance * rows) >= first, 0.0, FLOOR_SCORE
            )

    def key_values(count):
        def column_tile(index, carry):
            cols = pl.ds(pl.multiple_of(index * 256, 256), 256)
            normed = xn[0:count * rows, :]
            kb[0:count * rows, cols] = jnp.dot(
                normed, wk[:, cols], preferred_element_type=F32
            ).astype(BF16)
            vb[0:count * rows, cols] = jnp.dot(
                normed, wv[:, cols], preferred_element_type=F32
            ).astype(BF16)
            return carry

        lax.fori_loop(0, width // 256, column_tile, 0)

    def attend(count, bias_view, opening):
        keys = count * rows

        def pair_step(pair, carry):
            cols = pl.ds(pl.multiple_of(pair * 128, 128), 128)
            shade = bias_view()
            scores = lax.dot_general(
                q2[:, cols], kb[0:keys, cols], (((1,), (1,)), ((), ())),
                preferred_element_type=F32,
            ) + jnp.concatenate([shade, shade], axis=0)
            top = jnp.broadcast_to(
                jnp.max(scores, axis=-1, keepdims=True), (2 * rows, 128)
            )
            if not opening:
                before = mx[pair]
                top = jnp.maximum(top, before)
            weights16 = jnp.exp(scores - jnp.tile(top, (1, keys // 128))).astype(BF16)
            values = jnp.concatenate(
                [vb[0:keys, cols], jnp.ones((keys, 128), BF16)], axis=1
            )
            summed = jnp.dot(weights16, values, preferred_element_type=F32)
            if not opening:
                summed = summed + acc[pair] * jnp.tile(jnp.exp(before - top), (1, 2))
            acc[pair] = summed
            mx[pair] = top
            return carry

        lax.fori_loop(0, pairs, pair_step, 0)

    gain = na_ref[...]
    xn[0:rows, :] = layer_norm(x_ref[...].astype(F32), gain).astype(BF16)

    weights[0].wait()

    def query_tile(index, carry):
        cols = pl.ds(pl.multiple_of(index * 256, 256), 256)
        query = jnp.dot(xn[0:rows, :], wq[:, cols], preferred_element_type=F32)
        query = query.astype(BF16).astype(F32) * (HD ** -0.5)
        low = lax.broadcasted_iota(jnp.int32, (rows, 256), 1) % 128 < HD
        q2[0:rows, cols] = jnp.where(low, query, 0.0).astype(BF16)
        q2[rows:2 * rows, cols] = jnp.where(low, 0.0, query).astype(BF16)
        return carry

    lax.fori_loop(0, width // 256, query_tile, 0)
    weights[1].wait()
    weights[2].wait()
    key_values(1)

    def relay_first(part):
        wait_here(B, part)
        start(D, part)
        start(H, part)
        wait_here(A, part)
        start(F, part)
        start(E, part)

    def relay_second(part):
        wait_here(F, part)
        start(I, part)
        start(G, part)

    attend(1, lambda: bias_own[...], True)
    for part in range(PIECES):
        relay_first(part)

    def remote(slot, count):
        for index in range(count):
            xn[index * rows:(index + 1) * rows, :] = layer_norm(
                xb[slot + index].astype(F32), gain
            ).astype(BF16)
        key_values(count)
        attend(count, lambda: bias[:, slot * rows:(slot + count) * rows], False)

    remote(0, 1)
    for part in range(PIECES):
        relay_second(part)
    remote(1, 1)
    for event in (C, D, E, G, H, I):
        for part in range(PIECES):
            wait_here(event, part)
    remote(2, 3)

    low = lax.broadcasted_iota(jnp.int32, (rows, 128), 1) < HD

    def close_pair(pair, carry):
        cols = pl.ds(pl.multiple_of(pair * 128, 128), 128)
        state = acc[pair]
        total = jnp.where(low, state[0:rows, 0:128], state[rows:2 * rows, 0:128])
        weight_sum = jnp.where(low, state[0:rows, 128:256], state[rows:2 * rows, 128:256])
        heads[:, cols] = (total / weight_sum).astype(BF16)
        return carry

    lax.fori_loop(0, pairs, close_pair, 0)
    weights[3].wait()

    def output_tile(index, carry):
        cols = pl.ds(pl.multiple_of(index * 256, 256), 256)
        res[:, cols] = (
            x_ref[:, cols].astype(F32)
            + jnp.dot(heads[...], wo[:, cols], preferred_element_type=F32)
        ).astype(BF16)
        return carry

    lax.fori_loop(0, width // 256, output_tile, 0)
    xn[0:rows, :] = layer_norm(res[...].astype(F32), nc_ref[...]).astype(BF16)
    weights[4].wait()

    def unit_tile(index, carry):
        cols = pl.ds(pl.multiple_of(index * 256, 256), 256)
        gate_cols = pl.ds(pl.multiple_of(width + index * 256, 256), 256)
        normed = xn[0:rows, :]
        value = jnp.dot(normed, wg[:, cols], preferred_element_type=F32)
        gate = jnp.dot(normed, wg[:, gate_cols], preferred_element_type=F32)
        gated = (value * jax.nn.sigmoid(gate)).astype(BF16)
        gb[:, cols] = gated
        gext[32:32 + rows, cols] = gated.astype(F32)
        return carry

    lax.fori_loop(0, width // 256, unit_tile, 0)

    rim = pltpu.make_async_remote_copy(
        src_ref=gb.at[pl.ds(rows - 32, 32)],
        dst_ref=halo,
        send_sem=halo_sem.at[0],
        recv_sem=halo_sem.at[1],
        device_id={"seq": me + 1},
        device_id_type=MESH,
    )

    @pl.when(me + 1 < n)
    def _():
        rim.start()

    chunk = 64

    def depth_tile(base, cols):
        back = (
            lax.broadcasted_iota(jnp.int32, (chunk, 128), 0).astype(F32) + float(base)
            - startb[pl.ds(base, chunk), :]
        )
        total = jnp.zeros((chunk, 128), F32)
        for tap in range(KW):
            piece_rows = gext[pl.ds(base + 2 + tap, chunk), cols]
            kept = jnp.where(back >= float(KW - 1 - tap), piece_rows, 0.0)
            total = total + kept * wd_ref[tap:tap + 1, cols]
        depth[pl.ds(base, chunk), cols] = total

    def interior(index, carry):
        cols = pl.ds(pl.multiple_of(index * 128, 128), 128)
        for base in range(chunk, rows, chunk):
            depth_tile(base, cols)
        return carry

    lax.fori_loop(0, pairs, interior, 0)

    def finish(low_row, count):
        normed_depth = layer_norm(depth[low_row:low_row + count, :], nd_ref[...])
        out_ref[low_row:low_row + count, :] = (
            res[low_row:low_row + count, :].astype(F32)
            + normed_depth * jax.nn.sigmoid(normed_depth)
        ).astype(BF16)

    finish(chunk, rows - chunk)

    @pl.when(me == 0)
    def _():
        halo[...] = jnp.zeros_like(halo)

    @pl.when(me > 0)
    def _():
        rim.wait_recv()

    gext[0:32, :] = halo[...].astype(F32)

    def edge(index, carry):
        depth_tile(0, pl.ds(pl.multiple_of(index * 128, 128), 128))
        return carry

    lax.fori_loop(0, pairs, edge, 0)
    finish(0, chunk)

    for event in range(9):
        for part in range(PIECES):
            wait_sent(event, part)

    @pl.when(me + 1 < n)
    def _():
        rim.wait_send()


def body(
    frames_in, rec_start, norm_attn, w_query, w_key, w_value, w_out, norm_conv, w_glu, w_depth,
    norm_depth,
):
    rows, width = frames_in.shape
    pairs = width // 128
    vmem = pl.BlockSpec(memory_space=pltpu.VMEM)
    hbm = pl.BlockSpec(memory_space=pl.ANY)
    square = pltpu.VMEM((width, width), BF16)
    return pl.pallas_call(
        kernel,
        out_shape=jax.ShapeDtypeStruct((rows, width), BF16),
        in_specs=[vmem] * 6 + [hbm] * 5,
        out_specs=vmem,
        scratch_shapes=[
            pltpu.VMEM((5, rows, width), BF16),
            square, square, square, square,
            pltpu.VMEM((width, 2 * width), BF16),
            pltpu.VMEM((3 * rows, width), BF16),
            pltpu.VMEM((2 * rows, width), BF16),
            pltpu.VMEM((3 * rows, width), BF16),
            pltpu.VMEM((3 * rows, width), BF16),
            pltpu.VMEM((rows, 5 * rows), F32),
            pltpu.VMEM((rows, rows), F32),
            pltpu.VMEM((rows, 128), F32),
            pltpu.VMEM((pairs, 2 * rows, 128), F32),
            pltpu.VMEM((pairs, 2 * rows, 256), F32),
            pltpu.VMEM((rows, width), BF16),
            pltpu.VMEM((rows, width), BF16),
            pltpu.VMEM((rows, width), BF16),
            pltpu.VMEM((32, width), BF16),
            pltpu.VMEM((rows + 32, width), F32),
            pltpu.VMEM((rows, width), F32),
            pltpu.SemaphoreType.DMA((5,)),
            pltpu.SemaphoreType.DMA((9, PIECES)),
            pltpu.SemaphoreType.DMA((9, PIECES)),
            pltpu.SemaphoreType.DMA((2,)),
        ],
        compiler_params=pltpu.CompilerParams(
            collective_id=0, has_side_effects=True, vmem_limit_bytes=60 * 1024 * 1024
        ),
    )(
        frames_in, rec_start.reshape(1, rows), norm_attn.reshape(1, width),
        norm_conv.reshape(1, width), norm_depth.reshape(1, width), w_depth,
        w_query, w_key, w_value, w_out, w_glu,
    )


def solution(mesh):
    return jax.shard_map(
        body,
        mesh=mesh,
        in_specs=(P(("groups", "seq"), None), P(("groups", "seq"))) + (P(),) * 9,
        out_specs=P(("groups", "seq"), None),
        check_vma=False,
    )
```

time: 200 us -> 58 us (0.29)
  waiting for transfers between devices: 80.6 us -> 0 us
  Pallas kernels: 0 us -> 55.9 us
  matrix products: 42.4 us -> 0 us
  local copies, waits for them, and re-layouts: 41.4 us -> 1.87 us
  other arithmetic: 22.4 us -> 0 us
  starting transfers between devices: 11.8 us -> 0 us
    ppermute x6 -> x0, waiting for transfers between devices: 80.6 us -> none  [passed_along(): return lax.ppermute(block, axis, route)]
    pallas_call x0 -> x1, Pallas kernels: none -> 55.9 us  [body(): pl.pallas_call(kernel, out_shape=jax.ShapeDtypeStruct((rows, width), BF16...]
    dot_general x11 -> x0, matrix products: 42.4 us -> none  [the longest x3 19.2 us: attend_block(): jnp.einsum('hqk,khd->qhd', weights, value_heads, preferred_element_type=j...]
    dynamic_slice x6 -> x0, local copies, waits for them, and re-layouts: 21.3 us -> none  [attend_block(): lax.dynamic_index_in_dim(key_blocks, block_index, 0, keepdims=False)]
    reduce_sum x8 -> x0, other arithmetic: 16.4 us -> none  [the longest x2 9.3 us: layer_norm(): center = entries - jnp.mean(entries, axis=-1, keepdims=True)]
    ppermute x6 -> x0, starting transfers between devices: 11.8 us -> none  [passed_along(): return lax.ppermute(block, axis, route)]
    dynamic_update_slice x5 -> x0, local copies, waits for them, and re-layouts: 5.32 us -> none  [advance_hop(): lax.dynamic_update_slice_in_dim(stored_pairs, moving_pairs[None], hop_cou...]
    slice x6 -> x0, local copies, waits for them, and re-layouts: 5.32 us -> none  [the longest x3 5.2 us: attend_block(): block_pairs[:, feature_width:].reshape(block_rows, head_count, HD)]
  transfers between devices with their start and end apart: 6 -> 0, of which waited for: 6 -> 0; matrix products, arithmetic and copies ran while one was open for 0% -> 0% of each run, Pallas kernels for 0% -> 0%
where the time goes in v1:
time: 58 us; the launch traced here: 57.8 us
  Pallas kernels  55.9 us (96%)
  local copies, waits for them, and re-layouts  1.87 us (3%)
    pallas_call x1, Pallas kernels, body(): pl.pallas_call(kernel, out_shape=jax.ShapeDtypeStruct((rows, width), BF16...  55.9 us
    unnamed x1, local copies, waits for them, and re-layouts  1.87 us

profile of v1, /device:TPU:8, one launch (start us, length us, event | category | flops | bytes accessed | tf_op | source)
XLA Modules:
  0.0 57.8 jit_solution(4875702871445366715)
XLA Ops:
  0.0 55.9 %shard_map.109 = bf16[256,1024]{1,0:T(8,128)(2,1)} custom-call(bf16[256,1024]{1,0:T(8,128)(2,1)} %x_ref.1, s32[1,256]{1,0:T(1,128)} %bitcast.7, f32[1,1024]{1,0:T(1,128)} %bitcast.4, f32[1,1024]{1,0:T(1,128)} %bitcast.5, f32[1,1024]{1,0:T(1,128)} %bitcast.6, f32[31,1024]{1,0:T(8,128)} %wd_ref.1, bf16[1024,1024]{1,0:T(8,128)(2,1)} %wq_hbm.1, ...), custom_call_target="tpu_custom_call" | custom-call | tf_op jit(solution)/shard_map/pallas_call | solution.py:357
  56.0 1.9 %copy.13 = bf16[256,1024]{1,0:T(8,128)(2,1)} copy(bf16[256,1024]{1,0:T(8,128)(2,1)} %shard_map.109) | data formatting | bytes 1048576

commit v2 on v1

--- a/solution.py
+++ b/solution.py
@@ -13,6 +13,9 @@
 BF16 = jnp.bfloat16
 MESH = pl.DeviceIdType.MESH
 PIECES = 2
+UNROLL = 4
+TILE = 512
+GROUPS = ((0, 1), (1, 1), (2, 3))
 PLACE = {4: 0, 2: 1, 1: 2, 3: 3, 5: 4}
 DISTANCE = (4, 2, 1, 3, 5)
 A, B, C, D, E, F, G, H, I = range(9)
@@ -28,7 +31,7 @@
     x_ref, start_ref, na_ref, nc_ref, nd_ref, wd_ref,
     wq_hbm, wk_hbm, wv_hbm, wo_hbm, wg_hbm,
     out_ref,
-    xb, wq, wk, wv, wo, wg, xn, q2, kb, vb, bias, bias_own, startb, mx, acc, heads,
+    xb, own, qx, kx, wq, wk, wv, wo, wg, xn, q2, kb, vb, bias_own, startb, mx, acc, heads,
     res, gb, halo, gext, depth,
     w_sem, send_sem, recv_sem, halo_sem,
 ):
@@ -54,7 +57,7 @@
 
     def move(event, part, source, target, distance):
         span = pl.ds(part * piece, piece)
-        src = x_ref.at[span] if source is None else xb.at[PLACE[source], span]
+        src = own.at[span] if source is None else xb.at[PLACE[source], span]
         return pltpu.make_async_remote_copy(
             src_ref=src,
             dst_ref=xb.at[PLACE[distance], span],
@@ -106,12 +109,6 @@
             def _():
                 move(event, part, None, me, distance).wait_recv()
 
-    for part in range(PIECES):
-        start(A, part)
-        start(B, part)
-    for part in range(PIECES):
-        start(C, part)
-
     weights = [
         pltpu.make_async_copy(src, dst, w_sem.at[index])
         for index, (src, dst) in enumerate(
@@ -120,6 +117,16 @@
     ]
     for copy in weights:
         copy.start()
+
+    gain = na_ref[...]
+    for part in range(PIECES):
+        own[part * piece:(part + 1) * piece, :] = layer_norm(
+            x_ref[part * piece:(part + 1) * piece, :].astype(F32), gain
+        ).astype(BF16)
+        start(A, part)
+        start(B, part)
+    for part in range(PIECES):
+        start(C, part)
 
     for distance in DISTANCE:
         @pl.when(me < distance)
@@ -135,16 +142,23 @@
         place = lane + float(tile * 128)
         seen = (place >= first) & (place <= row_index)
         bias_own[:, tile * 128:(tile + 1) * 128] = jnp.where(seen, 0.0, FLOOR_SCORE)
-        for slot, distance in enumerate(DISTANCE):
-            at = slot * rows + tile * 128
-            bias[:, at:at + 128] = jnp.where(
-                place - float(distance * rows) >= first, 0.0, FLOOR_SCORE
-            )
-
-    def key_values(count):
+
+    head = jnp.broadcast_to(startb[0:1, :], (rows, 128))
+    flags = jnp.where(
+        lane == 0.0, jnp.where(first == head, 0.0, FLOOR_SCORE), jnp.where(lane == 1.0, 1.0, 0.0)
+    ).astype(BF16)
+    qx[0:rows, :] = flags
+    qx[rows:2 * rows, :] = flags
+    for slot, distance in enumerate(DISTANCE):
+        hidden = jnp.where(row_index - float(distance * rows) >= head, 0.0, FLOOR_SCORE)
+        kx[slot * rows:(slot + 1) * rows, :] = jnp.where(
+            lane == 0.0, 1.0, jnp.where(lane == 1.0, hidden, 0.0)
+        ).astype(BF16)
+
+    def key_values(source, count):
         def column_tile(index, carry):
-            cols = pl.ds(pl.multiple_of(index * 256, 256), 256)
-            normed = xn[0:count * rows, :]
+            cols = pl.ds(pl.multiple_of(index * TILE, TILE), TILE)
+            normed = source()
             kb[0:count * rows, cols] = jnp.dot(
                 normed, wk[:, cols], preferred_element_type=F32
             ).astype(BF16)
@@ -153,18 +167,24 @@
             ).astype(BF16)
             return carry
 
-        lax.fori_loop(0, width // 256, column_tile, 0)
-
-    def attend(count, bias_view, opening):
+        lax.fori_loop(0, width // TILE, column_tile, 0)
+
+    def attend(slot, count):
         keys = count * rows
+        opening = slot is None
 
         def pair_step(pair, carry):
             cols = pl.ds(pl.multiple_of(pair * 128, 128), 128)
-            shade = bias_view()
+            query, key = q2[:, cols], kb[0:keys, cols]
+            if not opening:
+                query = jnp.concatenate([query, qx[...]], axis=1)
+                key = jnp.concatenate([key, kx[slot * rows:slot * rows + keys, :]], axis=1)
             scores = lax.dot_general(
-                q2[:, cols], kb[0:keys, cols], (((1,), (1,)), ((), ())),
-                preferred_element_type=F32,
-            ) + jnp.concatenate([shade, shade], axis=0)
+                query, key, (((1,), (1,)), ((), ())), preferred_element_type=F32
+            )
+            if opening:
+                shade = bias_own[...]
+                scores = scores + jnp.concatenate([shade, shade], axis=0)
             top = jnp.broadcast_to(
                 jnp.max(scores, axis=-1, keepdims=True), (2 * rows, 128)
             )
@@ -182,16 +202,13 @@
             mx[pair] = top
             return carry
 
-        lax.fori_loop(0, pairs, pair_step, 0)
-
-    gain = na_ref[...]
-    xn[0:rows, :] = layer_norm(x_ref[...].astype(F32), gain).astype(BF16)
+        lax.fori_loop(0, pairs, pair_step, 0, unroll=UNROLL)
 
     weights[0].wait()
 
     def query_tile(index, carry):
         cols = pl.ds(pl.multiple_of(index * 256, 256), 256)
-        query = jnp.dot(xn[0:rows, :], wq[:, cols], preferred_element_type=F32)
+        query = jnp.dot(own[...], wq[:, cols], preferred_element_type=F32)
         query = query.astype(BF16).astype(F32) * (HD ** -0.5)
         low = lax.broadcasted_iota(jnp.int32, (rows, 256), 1) % 128 < HD
         q2[0:rows, cols] = jnp.where(low, query, 0.0).astype(BF16)
@@ -201,7 +218,7 @@
     lax.fori_loop(0, width // 256, query_tile, 0)
     weights[1].wait()
     weights[2].wait()
-    key_values(1)
+    key_values(lambda: own[...], 1)
 
     def relay_first(part):
         wait_here(B, part)
@@ -216,26 +233,25 @@
         start(I, part)
         start(G, part)
 
-    attend(1, lambda: bias_own[...], True)
+    attend(None, 1)
     for part in range(PIECES):
         relay_first(part)
 
     def remote(slot, count):
-        for index in range(count):
-            xn[index * rows:(index + 1) * rows, :] = layer_norm(
-                xb[slot + index].astype(F32), gain
-            ).astype(BF16)
-        key_values(count)
-        attend(count, lambda: bias[:, slot * rows:(slot + count) * rows], False)
-
-    remote(0, 1)
-    for part in range(PIECES):
-        relay_second(part)
-    remote(1, 1)
-    for event in (C, D, E, G, H, I):
-        for part in range(PIECES):
-            wait_here(event, part)
-    remote(2, 3)
+        key_values(
+            lambda: xb[slot:slot + count].reshape(count * rows, width), count
+        )
+        attend(slot, count)
+
+    for turn, (slot, count) in enumerate(GROUPS):
+        if turn == len(GROUPS) - 2:
+            for part in range(PIECES):
+                relay_second(part)
+        if turn == len(GROUPS) - 1:
+            for event in (C, D, E, G, H, I):
+                for part in range(PIECES):
+                    wait_here(event, part)
+        remote(slot, count)
 
     low = lax.broadcasted_iota(jnp.int32, (rows, 128), 1) < HD
 
@@ -361,13 +377,15 @@
         out_specs=vmem,
         scratch_shapes=[
             pltpu.VMEM((5, rows, width), BF16),
+            pltpu.VMEM((rows, width), BF16),
+            pltpu.VMEM((2 * rows, 128), BF16),
+            pltpu.VMEM((5 * rows, 128), BF16),
             square, square, square, square,
             pltpu.VMEM((width, 2 * width), BF16),
-            pltpu.VMEM((3 * rows, width), BF16),
+            pltpu.VMEM((rows, width), BF16),
             pltpu.VMEM((2 * rows, width), BF16),
             pltpu.VMEM((3 * rows, width), BF16),
             pltpu.VMEM((3 * rows, width), BF16),
-            pltpu.VMEM((rows, 5 * rows), F32),
             pltpu.VMEM((rows, rows), F32),
             pltpu.VMEM((rows, 128), F32),
             pltpu.VMEM((pairs, 2 * rows, 128), F32),

time: 58 us -> 49.1 us (0.85)
  Pallas kernels: 55.9 us -> 47.1 us
    pallas_call x1, Pallas kernels: 55.9 us -> 47.1 us  [body(): pl.pallas_call(kernel, out_shape=jax.ShapeDtypeStruct((rows, width), BF16...]
where the time goes in v2:
time: 49.1 us; the launch traced here: 49 us
  Pallas kernels  47.1 us (96%)
  local copies, waits for them, and re-layouts  1.87 us (4%)
    pallas_call x1, Pallas kernels, body(): pl.pallas_call(kernel, out_shape=jax.ShapeDtypeStruct((rows, width), BF16...  47.1 us
    unnamed x1, local copies, waits for them, and re-layouts  1.87 us

profile of v2, /device:TPU:8, one launch (start us, length us, event | category | flops | bytes accessed | tf_op | source)
XLA Modules:
  0.0 49.0 jit_solution(16402650127496025542)
XLA Ops:
  0.0 47.1 %shard_map.109 = bf16[256,1024]{1,0:T(8,128)(2,1)} custom-call(bf16[256,1024]{1,0:T(8,128)(2,1)} %x_ref.1, s32[1,256]{1,0:T(1,128)} %bitcast.7, f32[1,1024]{1,0:T(1,128)} %bitcast.4, f32[1,1024]{1,0:T(1,128)} %bitcast.5, f32[1,1024]{1,0:T(1,128)} %bitcast.6, f32[31,1024]{1,0:T(8,128)} %wd_ref.1, bf16[1024,1024]{1,0:T(8,128)(2,1)} %wq_hbm.1, ...), custom_call_target="tpu_custom_call" | custom-call | tf_op jit(solution)/shard_map/pallas_call | solution.py:373
  47.1 1.9 %copy.13 = bf16[256,1024]{1,0:T(8,128)(2,1)} copy(bf16[256,1024]{1,0:T(8,128)(2,1)} %shard_map.109) | data formatting | bytes 1048576

commit v3 on v2

--- a/solution.py
+++ b/solution.py
@@ -12,10 +12,10 @@
 F32 = jnp.float32
 BF16 = jnp.bfloat16
 MESH = pl.DeviceIdType.MESH
-PIECES = 2
-UNROLL = 4
+PIECES = 4
+UNROLL = 8
 TILE = 512
-GROUPS = ((0, 1), (1, 1), (2, 3))
+GROUPS = ((0, 1), (1, 1), (2, 2), (4, 1))
 PLACE = {4: 0, 2: 1, 1: 2, 3: 3, 5: 4}
 DISTANCE = (4, 2, 1, 3, 5)
 A, B, C, D, E, F, G, H, I = range(9)
@@ -233,8 +233,9 @@
         start(I, part)
         start(G, part)
 
+    relay_first(0)
     attend(None, 1)
-    for part in range(PIECES):
+    for part in range(1, PIECES):
         relay_first(part)
 
     def remote(slot, count):
@@ -244,11 +245,12 @@
         attend(slot, count)
 
     for turn, (slot, count) in enumerate(GROUPS):
-        if turn == len(GROUPS) - 2:
+        if turn == 1:
             for part in range(PIECES):
                 relay_second(part)
-        if turn == len(GROUPS) - 1:
-            for event in (C, D, E, G, H, I):
+        arrivals = {2: (C, D, E, G), 3: (H, I)} if len(GROUPS) == 4 else {2: (C, D, E, G, H, I)}
+        if turn in arrivals:
+            for event in arrivals[turn]:
                 for part in range(PIECES):
                     wait_here(event, part)
         remote(slot, count)

time: 49.1 us -> 46.4 us (0.945)
  Pallas kernels: 47.1 us -> 44.3 us
    pallas_call x1, Pallas kernels: 47.1 us -> 44.3 us  [body(): pl.pallas_call(kernel, out_shape=jax.ShapeDtypeStruct((rows, width), BF16...]
where the time goes in v3:
time: 46.4 us; the launch traced here: 46.2 us
  Pallas kernels  44.3 us (95%)
  local copies, waits for them, and re-layouts  1.87 us (4%)
    pallas_call x1, Pallas kernels, body(): pl.pallas_call(kernel, out_shape=jax.ShapeDtypeStruct((rows, width), BF16...  44.3 us
    unnamed x1, local copies, waits for them, and re-layouts  1.87 us

profile of v3, /device:TPU:8, one launch (start us, length us, event | category | flops | bytes accessed | tf_op | source)
XLA Modules:
  0.0 46.2 jit_solution(16112512313142507356)
XLA Ops:
  0.0 44.3 %shard_map.109 = bf16[256,1024]{1,0:T(8,128)(2,1)} custom-call(bf16[256,1024]{1,0:T(8,128)(2,1)} %x_ref.1, s32[1,256]{1,0:T(1,128)} %bitcast.7, f32[1,1024]{1,0:T(1,128)} %bitcast.4, f32[1,1024]{1,0:T(1,128)} %bitcast.5, f32[1,1024]{1,0:T(1,128)} %bitcast.6, f32[31,1024]{1,0:T(8,128)} %wd_ref.1, bf16[1024,1024]{1,0:T(8,128)(2,1)} %wq_hbm.1, ...), custom_call_target="tpu_custom_call" | custom-call | tf_op jit(solution)/shard_map/pallas_call | solution.py:375
  44.3 1.9 %copy.13 = bf16[256,1024]{1,0:T(8,128)(2,1)} copy(bf16[256,1024]{1,0:T(8,128)(2,1)} %shard_map.109) | data formatting | bytes 1048576
